TPU v7x, 128 devices: a whole 4x4x4 slice. The times are simulated.
128 devices in a mesh: grp: 4 (over y), row: 32 (over x, z, core).
Axes of the slice: x: 4, y: 4, z: 4, core: 2. Of those that a mesh axis runs over, the one named last changes fastest.
Arguments:
- b_tensor: bfloat16 [9984, 8, 768], P(None, 'grp', 'row'), may hold values from -0.21875 to 0.21875
- aux_counts: int32 [4], replicated, may hold values from 1 to 2, as said below
Outputs:
- exchange_matrix: float32 [9984, 9984], P('row', 'grp')
Inputs may be any that keep to these rules, and one draw needn't show every extreme that they name: `aux_counts`: some group has all 2 slots live.
All inputs are finite; a program needn't handle non-finite values.
Results may differ from a plain program's by a relative error of at most 0.0003.
Values may be sent and summed in bfloat16 or wider, within the bound.
No kernel may reach another device: no remote copies, remote signals or barrier semaphores. Data moves between devices by JAX's collectives and lax.ppermute only.
A program may use at most 128 MiB of HBM per device.

v0:
```python
import jax
import jax.numpy as jnp
from jax import lax
from jax.sharding import PartitionSpec as P


def shifted(block, axis, distance):
    devices = range(lax.axis_size(axis))
    route = [((i - distance) % len(devices), i) for i in devices]
    return lax.ppermute(block, axis, route)


def shards(b_tensor, aux_counts):
    row_count = lax.axis_size("row")
    row_rank = lax.axis_index("row")
    group_index = lax.axis_index("grp")
    slot_count = b_tensor.shape[1]
    live_count = lax.dynamic_index_in_dim(aux_counts, group_index, 0, keepdims=False)
    live_mask = (jnp.arange(slot_count) < live_count).astype(jnp.bfloat16)
    masked = b_tensor * live_mask[None, :, None]
    regrouped = lax.all_to_all(masked, "row", split_axis=0, concat_axis=2, tiled=True)
    block_size = regrouped.shape[0]
    own_rows = regrouped.reshape(block_size, -1)

    def tile_with(visitor):
        return lax.dot_general(
            own_rows, visitor, (((1,), (1,)), ((), ())), preferred_element_type=jnp.float32
        )

    upper_part = jnp.zeros((block_size, row_count, block_size), jnp.float32)
    upper_part = lax.dynamic_update_index_in_dim(upper_part, tile_with(own_rows), row_rank, 1)

    def advance(cycle_step, state_tuple):
        visiting, upper_acc = state_tuple
        visiting = shifted(visiting, "row", -1)
        target = (row_rank + cycle_step) % row_count
        upper_acc = lax.dynamic_update_index_in_dim(upper_acc, tile_with(visiting), target, 1)
        return (visiting, upper_acc)

    visiting, upper_part = lax.fori_loop(1, row_count, advance, (own_rows, upper_part))
    partial_value = upper_part.reshape(block_size, row_count * block_size)
    return lax.psum_scatter(partial_value, "grp", scatter_dimension=1, tiled=True)


def solution(mesh):
    return jax.shard_map(
        shards,
        mesh=mesh,
        in_specs=(P(None, "grp", "row"), P()),
        out_specs=P("row", "grp"),
        check_vma=False,
    )
```

profile of v0, /device:TPU:1, one launch (start us, length us, event | category | flops | bytes accessed | tf_op | source)
XLA Modules:
  0.0 851.2 jit_solution(9750454119854476417)
XLA Ops:
  17.7 16.5 %reshape.17 = bf16[32,2,7488]{2,1,0:T(2,128)(2,1)} reshape(bf16[9984,2,24]{2,1,0:T(2,128)(2,1)} %copy.14) | data formatting | bytes 1916928
  43.7 16.0 %all-to-all-done = bf16[32,2,7488]{2,1,0:T(2,128)(2,1)S(1)} async-done(((bf16[32,2,7488]{2,1,0:T(2,128)(2,1)}), bf16[32,2,7488]{2,1,0:T(2,128)(2,1)S(1)}, u32[]{:S(2)}, u32[]{:S(2)}) %all-to-all-start) | async-done | bytes 958496 | tf_op jit(solution)/shard_map/all_to_all | solution.py:21
  92.7 577.8 %while.17 = (s32[]{:T(128)}, bf16[312,1536]{1,0:T(8,128)(2,1)}, f32[312,32,312]{2,0,1:T(8,128)}, bf16[312,1536]{1,0:T(8,128)(2,1)S(1)}, s32[]{:T(128)}, /*index=5*/s32[]{:T(128)}, s32[]{:T(128)}, s32[]{:T(128)}, s32[]{:T(128)}) while((s32[]{:T(128)}, bf16[312,1536]{1,0:T(8,128)(2,1)}, f32[312,32,312]{2,0,1:T(8,128)}, ...), condition=%wide.region_1.2_spmd, body=%wide.region_0.1_spmd.sunk | while | flops 299040768 | bytes 8147236 | solution.py:40
  92.8 13.4 %collective-permute-done = bf16[312,1536]{1,0:T(8,128)(2,1)S(1)} collective-permute-done((bf16[312,1536]{1,0:T(8,128)(2,1)}, bf16[312,1536]{1,0:T(8,128)(2,1)S(1)}, u32[]{:S(2)}, u32[]{:S(2)}) %collective-permute-start) | collective-permute-done | bytes 958496 | tf_op jit(solution)/shard_map/while/body/eval_jaxpr/ppermute | solution.py:10
  172.1 13.6 %collective-permute-start = (bf16[312,1536]{1,0:T(8,128)(2,1)}, bf16[312,1536]{1,0:T(8,128)(2,1)S(1)}, u32[]{:S(2)}, u32[]{:S(2)}) collective-permute-start(bf16[312,1536]{1,0:T(8,128)(2,1)} %get-tuple-element.205), channel_id=1, source_target_pairs={{1,0},{2,1},{3,2},{4,3},{5,4},{6,5},{7,6},{8,7},{9,8},{10,9},{11,1... | collective-permute-start | bytes 2875400 | tf_op jit(solution)/shard_map/while/body/eval_jaxpr/ppermute | solution.py:10
  190.5 14.5 %collective-permute-start = (bf16[312,1536]{1,0:T(8,128)(2,1)}, bf16[312,1536]{1,0:T(8,128)(2,1)S(1)}, u32[]{:S(2)}, u32[]{:S(2)}) collective-permute-start(bf16[312,1536]{1,0:T(8,128)(2,1)} %get-tuple-element.205), channel_id=1, source_target_pairs={{1,0},{2,1},{3,2},{4,3},{5,4},{6,5},{7,6},{8,7},{9,8},{10,9},{11,1... | collective-permute-start | bytes 2875400 | tf_op jit(solution)/shard_map/while/body/eval_jaxpr/ppermute | solution.py:10
  209.7 14.4 %collective-permute-start = (bf16[312,1536]{1,0:T(8,128)(2,1)}, bf16[312,1536]{1,0:T(8,128)(2,1)S(1)}, u32[]{:S(2)}, u32[]{:S(2)}) collective-permute-start(bf16[312,1536]{1,0:T(8,128)(2,1)} %get-tuple-element.205), channel_id=1, source_target_pairs={{1,0},{2,1},{3,2},{4,3},{5,4},{6,5},{7,6},{8,7},{9,8},{10,9},{11,1... | collective-permute-start | bytes 2875400 | tf_op jit(solution)/shard_map/while/body/eval_jaxpr/ppermute | solution.py:10
  228.9 14.4 %collective-permute-start = (bf16[312,1536]{1,0:T(8,128)(2,1)}, bf16[312,1536]{1,0:T(8,128)(2,1)S(1)}, u32[]{:S(2)}, u32[]{:S(2)}) collective-permute-start(bf16[312,1536]{1,0:T(8,128)(2,1)} %get-tuple-element.205), channel_id=1, source_target_pairs={{1,0},{2,1},{3,2},{4,3},{5,4},{6,5},{7,6},{8,7},{9,8},{10,9},{11,1... | collective-permute-start | bytes 2875400 | tf_op jit(solution)/shard_map/while/body/eval_jaxpr/ppermute | solution.py:10
  248.1 14.4 %collective-permute-start = (bf16[312,1536]{1,0:T(8,128)(2,1)}, bf16[312,1536]{1,0:T(8,128)(2,1)S(1)}, u32[]{:S(2)}, u32[]{:S(2)}) collective-permute-start(bf16[312,1536]{1,0:T(8,128)(2,1)} %get-tuple-element.205), channel_id=1, source_target_pairs={{1,0},{2,1},{3,2},{4,3},{5,4},{6,5},{7,6},{8,7},{9,8},{10,9},{11,1... | collective-permute-start | bytes 2875400 | tf_op jit(solution)/shard_map/while/body/eval_jaxpr/ppermute | solution.py:10
  267.3 14.4 %collective-permute-start = (bf16[312,1536]{1,0:T(8,128)(2,1)}, bf16[312,1536]{1,0:T(8,128)(2,1)S(1)}, u32[]{:S(2)}, u32[]{:S(2)}) collective-permute-start(bf16[312,1536]{1,0:T(8,128)(2,1)} %get-tuple-element.205), channel_id=1, source_target_pairs={{1,0},{2,1},{3,2},{4,3},{5,4},{6,5},{7,6},{8,7},{9,8},{10,9},{11,1... | collective-permute-start | bytes 2875400 | tf_op jit(solution)/shard_map/while/body/eval_jaxpr/ppermute | solution.py:10
  286.4 14.5 %collective-permute-start = (bf16[312,1536]{1,0:T(8,128)(2,1)}, bf16[312,1536]{1,0:T(8,128)(2,1)S(1)}, u32[]{:S(2)}, u32[]{:S(2)}) collective-permute-start(bf16[312,1536]{1,0:T(8,128)(2,1)} %get-tuple-element.205), channel_id=1, source_target_pairs={{1,0},{2,1},{3,2},{4,3},{5,4},{6,5},{7,6},{8,7},{9,8},{10,9},{11,1... | collective-permute-start | bytes 2875400 | tf_op jit(solution)/shard_map/while/body/eval_jaxpr/ppermute | solution.py:10
  305.7 14.4 %collective-permute-start = (bf16[312,1536]{1,0:T(8,128)(2,1)}, bf16[312,1536]{1,0:T(8,128)(2,1)S(1)}, u32[]{:S(2)}, u32[]{:S(2)}) collective-permute-start(bf16[312,1536]{1,0:T(8,128)(2,1)} %get-tuple-element.205), channel_id=1, source_target_pairs={{1,0},{2,1},{3,2},{4,3},{5,4},{6,5},{7,6},{8,7},{9,8},{10,9},{11,1... | collective-permute-start | bytes 2875400 | tf_op jit(solution)/shard_map/while/body/eval_jaxpr/ppermute | solution.py:10
  324.9 14.4 %collective-permute-start = (bf16[312,1536]{1,0:T(8,128)(2,1)}, bf16[312,1536]{1,0:T(8,128)(2,1)S(1)}, u32[]{:S(2)}, u32[]{:S(2)}) collective-permute-start(bf16[312,1536]{1,0:T(8,128)(2,1)} %get-tuple-element.205), channel_id=1, source_target_pairs={{1,0},{2,1},{3,2},{4,3},{5,4},{6,5},{7,6},{8,7},{9,8},{10,9},{11,1... | collective-permute-start | bytes 2875400 | tf_op jit(solution)/shard_map/while/body/eval_jaxpr/ppermute | solution.py:10
  344.1 14.4 %collective-permute-start = (bf16[312,1536]{1,0:T(8,128)(2,1)}, bf16[312,1536]{1,0:T(8,128)(2,1)S(1)}, u32[]{:S(2)}, u32[]{:S(2)}) collective-permute-start(bf16[312,1536]{1,0:T(8,128)(2,1)} %get-tuple-element.205), channel_id=1, source_target_pairs={{1,0},{2,1},{3,2},{4,3},{5,4},{6,5},{7,6},{8,7},{9,8},{10,9},{11,1... | collective-permute-start | bytes 2875400 | tf_op jit(solution)/shard_map/while/body/eval_jaxpr/ppermute | solution.py:10
  363.2 14.4 %collective-permute-start = (bf16[312,1536]{1,0:T(8,128)(2,1)}, bf16[312,1536]{1,0:T(8,128)(2,1)S(1)}, u32[]{:S(2)}, u32[]{:S(2)}) collective-permute-start(bf16[312,1536]{1,0:T(8,128)(2,1)} %get-tuple-element.205), channel_id=1, source_target_pairs={{1,0},{2,1},{3,2},{4,3},{5,4},{6,5},{7,6},{8,7},{9,8},{10,9},{11,1... | collective-permute-start | bytes 2875400 | tf_op jit(solution)/shard_map/while/body/eval_jaxpr/ppermute | solution.py:10
  382.5 14.4 %collective-permute-start = (bf16[312,1536]{1,0:T(8,128)(2,1)}, bf16[312,1536]{1,0:T(8,128)(2,1)S(1)}, u32[]{:S(2)}, u32[]{:S(2)}) collective-permute-start(bf16[312,1536]{1,0:T(8,128)(2,1)} %get-tuple-element.205), channel_id=1, source_target_pairs={{1,0},{2,1},{3,2},{4,3},{5,4},{6,5},{7,6},{8,7},{9,8},{10,9},{11,1... | collective-permute-start | bytes 2875400 | tf_op jit(solution)/shard_map/while/body/eval_jaxpr/ppermute | solution.py:10
  401.7 14.4 %collective-permute-start = (bf16[312,1536]{1,0:T(8,128)(2,1)}, bf16[312,1536]{1,0:T(8,128)(2,1)S(1)}, u32[]{:S(2)}, u32[]{:S(2)}) collective-permute-start(bf16[312,1536]{1,0:T(8,128)(2,1)} %get-tuple-element.205), channel_id=1, source_target_pairs={{1,0},{2,1},{3,2},{4,3},{5,4},{6,5},{7,6},{8,7},{9,8},{10,9},{11,1... | collective-permute-start | bytes 2875400 | tf_op jit(solution)/shard_map/while/body/eval_jaxpr/ppermute | solution.py:10
  420.9 14.4 %collective-permute-start = (bf16[312,1536]{1,0:T(8,128)(2,1)}, bf16[312,1536]{1,0:T(8,128)(2,1)S(1)}, u32[]{:S(2)}, u32[]{:S(2)}) collective-permute-start(bf16[312,1536]{1,0:T(8,128)(2,1)} %get-tuple-element.205), channel_id=1, source_target_pairs={{1,0},{2,1},{3,2},{4,3},{5,4},{6,5},{7,6},{8,7},{9,8},{10,9},{11,1... | collective-permute-start | bytes 2875400 | tf_op jit(solution)/shard_map/while/body/eval_jaxpr/ppermute | solution.py:10
  440.1 14.4 %collective-permute-start = (bf16[312,1536]{1,0:T(8,128)(2,1)}, bf16[312,1536]{1,0:T(8,128)(2,1)S(1)}, u32[]{:S(2)}, u32[]{:S(2)}) collective-permute-start(bf16[312,1536]{1,0:T(8,128)(2,1)} %get-tuple-element.205), channel_id=1, source_target_pairs={{1,0},{2,1},{3,2},{4,3},{5,4},{6,5},{7,6},{8,7},{9,8},{10,9},{11,1... | collective-permute-start | bytes 2875400 | tf_op jit(solution)/shard_map/while/body/eval_jaxpr/ppermute | solution.py:10
  459.3 14.5 %collective-permute-start = (bf16[312,1536]{1,0:T(8,128)(2,1)}, bf16[312,1536]{1,0:T(8,128)(2,1)S(1)}, u32[]{:S(2)}, u32[]{:S(2)}) collective-permute-start(bf16[312,1536]{1,0:T(8,128)(2,1)} %get-tuple-element.205), channel_id=1, source_target_pairs={{1,0},{2,1},{3,2},{4,3},{5,4},{6,5},{7,6},{8,7},{9,8},{10,9},{11,1... | collective-permute-start | bytes 2875400 | tf_op jit(solution)/shard_map/while/body/eval_jaxpr/ppermute | solution.py:10
  478.5 14.4 %collective-permute-start = (bf16[312,1536]{1,0:T(8,128)(2,1)}, bf16[312,1536]{1,0:T(8,128)(2,1)S(1)}, u32[]{:S(2)}, u32[]{:S(2)}) collective-permute-start(bf16[312,1536]{1,0:T(8,128)(2,1)} %get-tuple-element.205), channel_id=1, source_target_pairs={{1,0},{2,1},{3,2},{4,3},{5,4},{6,5},{7,6},{8,7},{9,8},{10,9},{11,1... | collective-permute-start | bytes 2875400 | tf_op jit(solution)/shard_map/while/body/eval_jaxpr/ppermute | solution.py:10
  497.7 14.5 %collective-permute-start = (bf16[312,1536]{1,0:T(8,128)(2,1)}, bf16[312,1536]{1,0:T(8,128)(2,1)S(1)}, u32[]{:S(2)}, u32[]{:S(2)}) collective-permute-start(bf16[312,1536]{1,0:T(8,128)(2,1)} %get-tuple-element.205), channel_id=1, source_target_pairs={{1,0},{2,1},{3,2},{4,3},{5,4},{6,5},{7,6},{8,7},{9,8},{10,9},{11,1... | collective-permute-start | bytes 2875400 | tf_op jit(solution)/shard_map/while/body/eval_jaxpr/ppermute | solution.py:10
  516.9 14.4 %collective-permute-start = (bf16[312,1536]{1,0:T(8,128)(2,1)}, bf16[312,1536]{1,0:T(8,128)(2,1)S(1)}, u32[]{:S(2)}, u32[]{:S(2)}) collective-permute-start(bf16[312,1536]{1,0:T(8,128)(2,1)} %get-tuple-element.205), channel_id=1, source_target_pairs={{1,0},{2,1},{3,2},{4,3},{5,4},{6,5},{7,6},{8,7},{9,8},{10,9},{11,1... | collective-permute-start | bytes 2875400 | tf_op jit(solution)/shard_map/while/body/eval_jaxpr/ppermute | solution.py:10
  536.1 14.4 %collective-permute-start = (bf16[312,1536]{1,0:T(8,128)(2,1)}, bf16[312,1536]{1,0:T(8,128)(2,1)S(1)}, u32[]{:S(2)}, u32[]{:S(2)}) collective-permute-start(bf16[312,1536]{1,0:T(8,128)(2,1)} %get-tuple-element.205), channel_id=1, source_target_pairs={{1,0},{2,1},{3,2},{4,3},{5,4},{6,5},{7,6},{8,7},{9,8},{10,9},{11,1... | collective-permute-start | bytes 2875400 | tf_op jit(solution)/shard_map/while/body/eval_jaxpr/ppermute | solution.py:10
  555.3 14.4 %collective-permute-start = (bf16[312,1536]{1,0:T(8,128)(2,1)}, bf16[312,1536]{1,0:T(8,128)(2,1)S(1)}, u32[]{:S(2)}, u32[]{:S(2)}) collective-permute-start(bf16[312,1536]{1,0:T(8,128)(2,1)} %get-tuple-element.205), channel_id=1, source_target_pairs={{1,0},{2,1},{3,2},{4,3},{5,4},{6,5},{7,6},{8,7},{9,8},{10,9},{11,1... | collective-permute-start | bytes 2875400 | tf_op jit(solution)/shard_map/while/body/eval_jaxpr/ppermute | solution.py:10
  574.6 14.4 %collective-permute-start = (bf16[312,1536]{1,0:T(8,128)(2,1)}, bf16[312,1536]{1,0:T(8,128)(2,1)S(1)}, u32[]{:S(2)}, u32[]{:S(2)}) collective-permute-start(bf16[312,1536]{1,0:T(8,128)(2,1)} %get-tuple-element.205), channel_id=1, source_target_pairs={{1,0},{2,1},{3,2},{4,3},{5,4},{6,5},{7,6},{8,7},{9,8},{10,9},{11,1... | collective-permute-start | bytes 2875400 | tf_op jit(solution)/shard_map/while/body/eval_jaxpr/ppermute | solution.py:10
  593.7 14.5 %collective-permute-start = (bf16[312,1536]{1,0:T(8,128)(2,1)}, bf16[312,1536]{1,0:T(8,128)(2,1)S(1)}, u32[]{:S(2)}, u32[]{:S(2)}) collective-permute-start(bf16[312,1536]{1,0:T(8,128)(2,1)} %get-tuple-element.205), channel_id=1, source_target_pairs={{1,0},{2,1},{3,2},{4,3},{5,4},{6,5},{7,6},{8,7},{9,8},{10,9},{11,1... | collective-permute-start | bytes 2875400 | tf_op jit(solution)/shard_map/while/body/eval_jaxpr/ppermute | solution.py:10
  612.9 14.4 %collective-permute-start = (bf16[312,1536]{1,0:T(8,128)(2,1)}, bf16[312,1536]{1,0:T(8,128)(2,1)S(1)}, u32[]{:S(2)}, u32[]{:S(2)}) collective-permute-start(bf16[312,1536]{1,0:T(8,128)(2,1)} %get-tuple-element.205), channel_id=1, source_target_pairs={{1,0},{2,1},{3,2},{4,3},{5,4},{6,5},{7,6},{8,7},{9,8},{10,9},{11,1... | collective-permute-start | bytes 2875400 | tf_op jit(solution)/shard_map/while/body/eval_jaxpr/ppermute | solution.py:10
  632.1 14.5 %collective-permute-start = (bf16[312,1536]{1,0:T(8,128)(2,1)}, bf16[312,1536]{1,0:T(8,128)(2,1)S(1)}, u32[]{:S(2)}, u32[]{:S(2)}) collective-permute-start(bf16[312,1536]{1,0:T(8,128)(2,1)} %get-tuple-element.205), channel_id=1, source_target_pairs={{1,0},{2,1},{3,2},{4,3},{5,4},{6,5},{7,6},{8,7},{9,8},{10,9},{11,1... | collective-permute-start | bytes 2875400 | tf_op jit(solution)/shard_map/while/body/eval_jaxpr/ppermute | solution.py:10
  651.3 14.4 %collective-permute-start = (bf16[312,1536]{1,0:T(8,128)(2,1)}, bf16[312,1536]{1,0:T(8,128)(2,1)S(1)}, u32[]{:S(2)}, u32[]{:S(2)}) collective-permute-start(bf16[312,1536]{1,0:T(8,128)(2,1)} %get-tuple-element.205), channel_id=1, source_target_pairs={{1,0},{2,1},{3,2},{4,3},{5,4},{6,5},{7,6},{8,7},{9,8},{10,9},{11,1... | collective-permute-start | bytes 2875400 | tf_op jit(solution)/shard_map/while/body/eval_jaxpr/ppermute | solution.py:10
  670.5 16.9 %copy.25 = f32[312,32,312]{0,2,1:T(8,128)} copy(f32[312,32,312]{2,0,1:T(8,128)} %get-tuple-element.138) | data formatting | bytes 24920064
  687.5 151.8 %reduce-scatter.4.cloned.1.call-done = f32[2496,312]{1,0:T(8,128)} async-done(((f32[9984,312]{1,0:T(8,128)}), f32[2496,312]{1,0:T(8,128)}) %reduce-scatter.4.cloned.1.call-update) | async-done | bytes 3115024
  (114 shorter events, 248.9 us)
Async XLA Ops:
  34.2 25.5 %all-to-all-start = ((bf16[32,2,7488]{2,1,0:T(2,128)(2,1)}), bf16[32,2,7488]{2,1,0:T(2,128)(2,1)S(1)}, u32[]{:S(2)}, u32[]{:S(2)}) async-start(bf16[32,2,7488]{2,1,0:T(2,128)(2,1)} %reshape.17), calls=%async_computation | async-start | bytes 1933312 | tf_op jit(solution)/shard_map/all_to_all | solution.py:21
  43.6 795.6 %reduce-scatter.4.cloned.1.call-start = ((), (), s32[]{:S(2)}) async-start(), calls=%async_computation.2 | async-start | bytes 19169280
  92.7 13.5 %collective-permute-start = (bf16[312,1536]{1,0:T(8,128)(2,1)}, bf16[312,1536]{1,0:T(8,128)(2,1)S(1)}, u32[]{:S(2)}, u32[]{:S(2)}) collective-permute-start(bf16[312,1536]{1,0:T(8,128)(2,1)} %get-tuple-element.205), channel_id=1, source_target_pairs={{1,0},{2,1},{3,2},{4,3},{5,4},{6,5},{7,6},{8,7},{9,8},{10,9},{11,1... | collective-permute-start | bytes 2875400 | tf_op jit(solution)/shard_map/while/body/eval_jaxpr/ppermute | solution.py:10
  108.6 13.5 %collective-permute-start = (bf16[312,1536]{1,0:T(8,128)(2,1)}, bf16[312,1536]{1,0:T(8,128)(2,1)S(1)}, u32[]{:S(2)}, u32[]{:S(2)}) collective-permute-start(bf16[312,1536]{1,0:T(8,128)(2,1)} %get-tuple-element.205), channel_id=1, source_target_pairs={{1,0},{2,1},{3,2},{4,3},{5,4},{6,5},{7,6},{8,7},{9,8},{10,9},{11,1... | collective-permute-start | bytes 2875400 | tf_op jit(solution)/shard_map/while/body/eval_jaxpr/ppermute | solution.py:10
  124.5 13.5 %collective-permute-start = (bf16[312,1536]{1,0:T(8,128)(2,1)}, bf16[312,1536]{1,0:T(8,128)(2,1)S(1)}, u32[]{:S(2)}, u32[]{:S(2)}) collective-permute-start(bf16[312,1536]{1,0:T(8,128)(2,1)} %get-tuple-element.205), channel_id=1, source_target_pairs={{1,0},{2,1},{3,2},{4,3},{5,4},{6,5},{7,6},{8,7},{9,8},{10,9},{11,1... | collective-permute-start | bytes 2875400 | tf_op jit(solution)/shard_map/while/body/eval_jaxpr/ppermute | solution.py:10
  156.2 13.5 %collective-permute-start = (bf16[312,1536]{1,0:T(8,128)(2,1)}, bf16[312,1536]{1,0:T(8,128)(2,1)S(1)}, u32[]{:S(2)}, u32[]{:S(2)}) collective-permute-start(bf16[312,1536]{1,0:T(8,128)(2,1)} %get-tuple-element.205), channel_id=1, source_target_pairs={{1,0},{2,1},{3,2},{4,3},{5,4},{6,5},{7,6},{8,7},{9,8},{10,9},{11,1... | collective-permute-start | bytes 2875400 | tf_op jit(solution)/shard_map/while/body/eval_jaxpr/ppermute | solution.py:10
  172.1 16.0 %collective-permute-start = (bf16[312,1536]{1,0:T(8,128)(2,1)}, bf16[312,1536]{1,0:T(8,128)(2,1)S(1)}, u32[]{:S(2)}, u32[]{:S(2)}) collective-permute-start(bf16[312,1536]{1,0:T(8,128)(2,1)} %get-tuple-element.205), channel_id=1, source_target_pairs={{1,0},{2,1},{3,2},{4,3},{5,4},{6,5},{7,6},{8,7},{9,8},{10,9},{11,1... | collective-permute-start | bytes 2875400 | tf_op jit(solution)/shard_map/while/body/eval_jaxpr/ppermute | solution.py:10
  190.5 16.8 %collective-permute-start = (bf16[312,1536]{1,0:T(8,128)(2,1)}, bf16[312,1536]{1,0:T(8,128)(2,1)S(1)}, u32[]{:S(2)}, u32[]{:S(2)}) collective-permute-start(bf16[312,1536]{1,0:T(8,128)(2,1)} %get-tuple-element.205), channel_id=1, source_target_pairs={{1,0},{2,1},{3,2},{4,3},{5,4},{6,5},{7,6},{8,7},{9,8},{10,9},{11,1... | collective-permute-start | bytes 2875400 | tf_op jit(solution)/shard_map/while/body/eval_jaxpr/ppermute | solution.py:10
  209.7 16.8 %collective-permute-start = (bf16[312,1536]{1,0:T(8,128)(2,1)}, bf16[312,1536]{1,0:T(8,128)(2,1)S(1)}, u32[]{:S(2)}, u32[]{:S(2)}) collective-permute-start(bf16[312,1536]{1,0:T(8,128)(2,1)} %get-tuple-element.205), channel_id=1, source_target_pairs={{1,0},{2,1},{3,2},{4,3},{5,4},{6,5},{7,6},{8,7},{9,8},{10,9},{11,1... | collective-permute-start | bytes 2875400 | tf_op jit(solution)/shard_map/while/body/eval_jaxpr/ppermute | solution.py:10
  228.9 16.8 %collective-permute-start = (bf16[312,1536]{1,0:T(8,128)(2,1)}, bf16[312,1536]{1,0:T(8,128)(2,1)S(1)}, u32[]{:S(2)}, u32[]{:S(2)}) collective-permute-start(bf16[312,1536]{1,0:T(8,128)(2,1)} %get-tuple-element.205), channel_id=1, source_target_pairs={{1,0},{2,1},{3,2},{4,3},{5,4},{6,5},{7,6},{8,7},{9,8},{10,9},{11,1... | collective-permute-start | bytes 2875400 | tf_op jit(solution)/shard_map/while/body/eval_jaxpr/ppermute | solution.py:10
  248.1 16.8 %collective-permute-start = (bf16[312,1536]{1,0:T(8,128)(2,1)}, bf16[312,1536]{1,0:T(8,128)(2,1)S(1)}, u32[]{:S(2)}, u32[]{:S(2)}) collective-permute-start(bf16[312,1536]{1,0:T(8,128)(2,1)} %get-tuple-element.205), channel_id=1, source_target_pairs={{1,0},{2,1},{3,2},{4,3},{5,4},{6,5},{7,6},{8,7},{9,8},{10,9},{11,1... | collective-permute-start | bytes 2875400 | tf_op jit(solution)/shard_map/while/body/eval_jaxpr/ppermute | solution.py:10
  267.3 16.8 %collective-permute-start = (bf16[312,1536]{1,0:T(8,128)(2,1)}, bf16[312,1536]{1,0:T(8,128)(2,1)S(1)}, u32[]{:S(2)}, u32[]{:S(2)}) collective-permute-start(bf16[312,1536]{1,0:T(8,128)(2,1)} %get-tuple-element.205), channel_id=1, source_target_pairs={{1,0},{2,1},{3,2},{4,3},{5,4},{6,5},{7,6},{8,7},{9,8},{10,9},{11,1... | collective-permute-start | bytes 2875400 | tf_op jit(solution)/shard_map/while/body/eval_jaxpr/ppermute | solution.py:10
  286.4 16.8 %collective-permute-start = (bf16[312,1536]{1,0:T(8,128)(2,1)}, bf16[312,1536]{1,0:T(8,128)(2,1)S(1)}, u32[]{:S(2)}, u32[]{:S(2)}) collective-permute-start(bf16[312,1536]{1,0:T(8,128)(2,1)} %get-tuple-element.205), channel_id=1, source_target_pairs={{1,0},{2,1},{3,2},{4,3},{5,4},{6,5},{7,6},{8,7},{9,8},{10,9},{11,1... | collective-permute-start | bytes 2875400 | tf_op jit(solution)/shard_map/while/body/eval_jaxpr/ppermute | solution.py:10
  305.7 16.8 %collective-permute-start = (bf16[312,1536]{1,0:T(8,128)(2,1)}, bf16[312,1536]{1,0:T(8,128)(2,1)S(1)}, u32[]{:S(2)}, u32[]{:S(2)}) collective-permute-start(bf16[312,1536]{1,0:T(8,128)(2,1)} %get-tuple-element.205), channel_id=1, source_target_pairs={{1,0},{2,1},{3,2},{4,3},{5,4},{6,5},{7,6},{8,7},{9,8},{10,9},{11,1... | collective-permute-start | bytes 2875400 | tf_op jit(solution)/shard_map/while/body/eval_jaxpr/ppermute | solution.py:10
  324.9 16.8 %collective-permute-start = (bf16[312,1536]{1,0:T(8,128)(2,1)}, bf16[312,1536]{1,0:T(8,128)(2,1)S(1)}, u32[]{:S(2)}, u32[]{:S(2)}) collective-permute-start(bf16[312,1536]{1,0:T(8,128)(2,1)} %get-tuple-element.205), channel_id=1, source_target_pairs={{1,0},{2,1},{3,2},{4,3},{5,4},{6,5},{7,6},{8,7},{9,8},{10,9},{11,1... | collective-permute-start | bytes 2875400 | tf_op jit(solution)/shard_map/while/body/eval_jaxpr/ppermute | solution.py:10
  344.1 16.8 %collective-permute-start = (bf16[312,1536]{1,0:T(8,128)(2,1)}, bf16[312,1536]{1,0:T(8,128)(2,1)S(1)}, u32[]{:S(2)}, u32[]{:S(2)}) collective-permute-start(bf16[312,1536]{1,0:T(8,128)(2,1)} %get-tuple-element.205), channel_id=1, source_target_pairs={{1,0},{2,1},{3,2},{4,3},{5,4},{6,5},{7,6},{8,7},{9,8},{10,9},{11,1... | collective-permute-start | bytes 2875400 | tf_op jit(solution)/shard_map/while/body/eval_jaxpr/ppermute | solution.py:10
  363.2 16.8 %collective-permute-start = (bf16[312,1536]{1,0:T(8,128)(2,1)}, bf16[312,1536]{1,0:T(8,128)(2,1)S(1)}, u32[]{:S(2)}, u32[]{:S(2)}) collective-permute-start(bf16[312,1536]{1,0:T(8,128)(2,1)} %get-tuple-element.205), channel_id=1, source_target_pairs={{1,0},{2,1},{3,2},{4,3},{5,4},{6,5},{7,6},{8,7},{9,8},{10,9},{11,1... | collective-permute-start | bytes 2875400 | tf_op jit(solution)/shard_map/while/body/eval_jaxpr/ppermute | solution.py:10
  382.5 16.8 %collective-permute-start = (bf16[312,1536]{1,0:T(8,128)(2,1)}, bf16[312,1536]{1,0:T(8,128)(2,1)S(1)}, u32[]{:S(2)}, u32[]{:S(2)}) collective-permute-start(bf16[312,1536]{1,0:T(8,128)(2,1)} %get-tuple-element.205), channel_id=1, source_target_pairs={{1,0},{2,1},{3,2},{4,3},{5,4},{6,5},{7,6},{8,7},{9,8},{10,9},{11,1... | collective-permute-start | bytes 2875400 | tf_op jit(solution)/shard_map/while/body/eval_jaxpr/ppermute | solution.py:10
  401.7 16.8 %collective-permute-start = (bf16[312,1536]{1,0:T(8,128)(2,1)}, bf16[312,1536]{1,0:T(8,128)(2,1)S(1)}, u32[]{:S(2)}, u32[]{:S(2)}) collective-permute-start(bf16[312,1536]{1,0:T(8,128)(2,1)} %get-tuple-element.205), channel_id=1, source_target_pairs={{1,0},{2,1},{3,2},{4,3},{5,4},{6,5},{7,6},{8,7},{9,8},{10,9},{11,1... | collective-permute-start | bytes 2875400 | tf_op jit(solution)/shard_map/while/body/eval_jaxpr/ppermute | solution.py:10
  420.9 16.8 %collective-permute-start = (bf16[312,1536]{1,0:T(8,128)(2,1)}, bf16[312,1536]{1,0:T(8,128)(2,1)S(1)}, u32[]{:S(2)}, u32[]{:S(2)}) collective-permute-start(bf16[312,1536]{1,0:T(8,128)(2,1)} %get-tuple-element.205), channel_id=1, source_target_pairs={{1,0},{2,1},{3,2},{4,3},{5,4},{6,5},{7,6},{8,7},{9,8},{10,9},{11,1... | collective-permute-start | bytes 2875400 | tf_op jit(solution)/shard_map/while/body/eval_jaxpr/ppermute | solution.py:10
  440.1 16.8 %collective-permute-start = (bf16[312,1536]{1,0:T(8,128)(2,1)}, bf16[312,1536]{1,0:T(8,128)(2,1)S(1)}, u32[]{:S(2)}, u32[]{:S(2)}) collective-permute-start(bf16[312,1536]{1,0:T(8,128)(2,1)} %get-tuple-element.205), channel_id=1, source_target_pairs={{1,0},{2,1},{3,2},{4,3},{5,4},{6,5},{7,6},{8,7},{9,8},{10,9},{11,1... | collective-permute-start | bytes 2875400 | tf_op jit(solution)/shard_map/while/body/eval_jaxpr/ppermute | solution.py:10
  459.3 16.8 %collective-permute-start = (bf16[312,1536]{1,0:T(8,128)(2,1)}, bf16[312,1536]{1,0:T(8,128)(2,1)S(1)}, u32[]{:S(2)}, u32[]{:S(2)}) collective-permute-start(bf16[312,1536]{1,0:T(8,128)(2,1)} %get-tuple-element.205), channel_id=1, source_target_pairs={{1,0},{2,1},{3,2},{4,3},{5,4},{6,5},{7,6},{8,7},{9,8},{10,9},{11,1... | collective-permute-start | bytes 2875400 | tf_op jit(solution)/shard_map/while/body/eval_jaxpr/ppermute | solution.py:10
  478.5 16.8 %collective-permute-start = (bf16[312,1536]{1,0:T(8,128)(2,1)}, bf16[312,1536]{1,0:T(8,128)(2,1)S(1)}, u32[]{:S(2)}, u32[]{:S(2)}) collective-permute-start(bf16[312,1536]{1,0:T(8,128)(2,1)} %get-tuple-element.205), channel_id=1, source_target_pairs={{1,0},{2,1},{3,2},{4,3},{5,4},{6,5},{7,6},{8,7},{9,8},{10,9},{11,1... | collective-permute-start | bytes 2875400 | tf_op jit(solution)/shard_map/while/body/eval_jaxpr/ppermute | solution.py:10
  497.7 16.8 %collective-permute-start = (bf16[312,1536]{1,0:T(8,128)(2,1)}, bf16[312,1536]{1,0:T(8,128)(2,1)S(1)}, u32[]{:S(2)}, u32[]{:S(2)}) collective-permute-start(bf16[312,1536]{1,0:T(8,128)(2,1)} %get-tuple-element.205), channel_id=1, source_target_pairs={{1,0},{2,1},{3,2},{4,3},{5,4},{6,5},{7,6},{8,7},{9,8},{10,9},{11,1... | collective-permute-start | bytes 2875400 | tf_op jit(solution)/shard_map/while/body/eval_jaxpr/ppermute | solution.py:10
  516.9 16.8 %collective-permute-start = (bf16[312,1536]{1,0:T(8,128)(2,1)}, bf16[312,1536]{1,0:T(8,128)(2,1)S(1)}, u32[]{:S(2)}, u32[]{:S(2)}) collective-permute-start(bf16[312,1536]{1,0:T(8,128)(2,1)} %get-tuple-element.205), channel_id=1, source_target_pairs={{1,0},{2,1},{3,2},{4,3},{5,4},{6,5},{7,6},{8,7},{9,8},{10,9},{11,1... | collective-permute-start | bytes 2875400 | tf_op jit(solution)/shard_map/while/body/eval_jaxpr/ppermute | solution.py:10
  536.1 16.8 %collective-permute-start = (bf16[312,1536]{1,0:T(8,128)(2,1)}, bf16[312,1536]{1,0:T(8,128)(2,1)S(1)}, u32[]{:S(2)}, u32[]{:S(2)}) collective-permute-start(bf16[312,1536]{1,0:T(8,128)(2,1)} %get-tuple-element.205), channel_id=1, source_target_pairs={{1,0},{2,1},{3,2},{4,3},{5,4},{6,5},{7,6},{8,7},{9,8},{10,9},{11,1... | collective-permute-start | bytes 2875400 | tf_op jit(solution)/shard_map/while/body/eval_jaxpr/ppermute | solution.py:10
  555.3 16.8 %collective-permute-start = (bf16[312,1536]{1,0:T(8,128)(2,1)}, bf16[312,1536]{1,0:T(8,128)(2,1)S(1)}, u32[]{:S(2)}, u32[]{:S(2)}) collective-permute-start(bf16[312,1536]{1,0:T(8,128)(2,1)} %get-tuple-element.205), channel_id=1, source_target_pairs={{1,0},{2,1},{3,2},{4,3},{5,4},{6,5},{7,6},{8,7},{9,8},{10,9},{11,1... | collective-permute-start | bytes 2875400 | tf_op jit(solution)/shard_map/while/body/eval_jaxpr/ppermute | solution.py:10
  574.6 16.7 %collective-permute-start = (bf16[312,1536]{1,0:T(8,128)(2,1)}, bf16[312,1536]{1,0:T(8,128)(2,1)S(1)}, u32[]{:S(2)}, u32[]{:S(2)}) collective-permute-start(bf16[312,1536]{1,0:T(8,128)(2,1)} %get-tuple-element.205), channel_id=1, source_target_pairs={{1,0},{2,1},{3,2},{4,3},{5,4},{6,5},{7,6},{8,7},{9,8},{10,9},{11,1... | collective-permute-start | bytes 2875400 | tf_op jit(solution)/shard_map/while/body/eval_jaxpr/ppermute | solution.py:10
  593.7 16.8 %collective-permute-start = (bf16[312,1536]{1,0:T(8,128)(2,1)}, bf16[312,1536]{1,0:T(8,128)(2,1)S(1)}, u32[]{:S(2)}, u32[]{:S(2)}) collective-permute-start(bf16[312,1536]{1,0:T(8,128)(2,1)} %get-tuple-element.205), channel_id=1, source_target_pairs={{1,0},{2,1},{3,2},{4,3},{5,4},{6,5},{7,6},{8,7},{9,8},{10,9},{11,1... | collective-permute-start | bytes 2875400 | tf_op jit(solution)/shard_map/while/body/eval_jaxpr/ppermute | solution.py:10
  612.9 16.7 %collective-permute-start = (bf16[312,1536]{1,0:T(8,128)(2,1)}, bf16[312,1536]{1,0:T(8,128)(2,1)S(1)}, u32[]{:S(2)}, u32[]{:S(2)}) collective-permute-start(bf16[312,1536]{1,0:T(8,128)(2,1)} %get-tuple-element.205), channel_id=1, source_target_pairs={{1,0},{2,1},{3,2},{4,3},{5,4},{6,5},{7,6},{8,7},{9,8},{10,9},{11,1... | collective-permute-start | bytes 2875400 | tf_op jit(solution)/shard_map/while/body/eval_jaxpr/ppermute | solution.py:10
  632.1 16.9 %collective-permute-start = (bf16[312,1536]{1,0:T(8,128)(2,1)}, bf16[312,1536]{1,0:T(8,128)(2,1)S(1)}, u32[]{:S(2)}, u32[]{:S(2)}) collective-permute-start(bf16[312,1536]{1,0:T(8,128)(2,1)} %get-tuple-element.205), channel_id=1, source_target_pairs={{1,0},{2,1},{3,2},{4,3},{5,4},{6,5},{7,6},{8,7},{9,8},{10,9},{11,1... | collective-permute-start | bytes 2875400 | tf_op jit(solution)/shard_map/while/body/eval_jaxpr/ppermute | solution.py:10
  651.3 16.8 %collective-permute-start = (bf16[312,1536]{1,0:T(8,128)(2,1)}, bf16[312,1536]{1,0:T(8,128)(2,1)S(1)}, u32[]{:S(2)}, u32[]{:S(2)}) collective-permute-start(bf16[312,1536]{1,0:T(8,128)(2,1)} %get-tuple-element.205), channel_id=1, source_target_pairs={{1,0},{2,1},{3,2},{4,3},{5,4},{6,5},{7,6},{8,7},{9,8},{10,9},{11,1... | collective-permute-start | bytes 2875400 | tf_op jit(solution)/shard_map/while/body/eval_jaxpr/ppermute | solution.py:10
  (2 other events, 18.9 us)
Sparse Core Ops, SparseCore 0:
  687.6 151.5 reduce-scatter.3
where the time goes:
time: 852 us; the launch traced here: 851 us
  starting transfers between devices  405 us (48%)
  waiting for transfers between devices  275 us (32%)
  local copies, waits for them, and re-layouts  109 us (13%)
  matrix products  46.3 us (5%)
  between operations  13.5 us (2%)
    ppermute x31, starting transfers between devices, shifted(): return lax.ppermute(block, axis, route)  396 us
    unnamed x2, waiting for transfers between devices  152 us
    ppermute x31, waiting for transfers between devices, shifted(): return lax.ppermute(block, axis, route)  108 us
    unnamed x7, local copies, waits for them, and re-layouts  51.1 us
    dot_general x32, matrix products, tile_with(): lax.dot_general(own_rows, visitor, (((1,), (1,)), ((), ())), preferred_el...  46.3 us
    while x31, local copies, waits for them, and re-layouts  29 us
    all_to_all x2, local copies, waits for them, and re-layouts, shards(): lax.all_to_all(masked, 'row', split_axis=0, concat_axis=2, tiled=True)  18.2 us
  transfers between devices with their start and end apart: 33, of which 33 were waited for; matrix products, arithmetic and copies ran while one was open for 0% of the time, Pallas kernels for 0%

commit v1 on v0

--- a/solution.py
+++ b/solution.py
@@ -2,6 +2,16 @@
 import jax.numpy as jnp
 from jax import lax
 from jax.sharding import PartitionSpec as P
+
+
+def map_refer(xin):
+    d_next = jnp.concatenate(
+        lax.all_to_all(
+            jnp.stack(jnp.split(xin, lax.axis_size("row"), axis=0), axis=0), "row", 0, 0
+        ),
+        axis=2,
+    )
+    return d_next
 
 
 def shifted(block, axis, distance):
@@ -18,7 +28,7 @@
     live_count = lax.dynamic_index_in_dim(aux_counts, group_index, 0, keepdims=False)
     live_mask = (jnp.arange(slot_count) < live_count).astype(jnp.bfloat16)
     masked = b_tensor * live_mask[None, :, None]
-    regrouped = lax.all_to_all(masked, "row", split_axis=0, concat_axis=2, tiled=True)
+    regrouped = map_refer(masked)
     block_size = regrouped.shape[0]
     own_rows = regrouped.reshape(block_size, -1)
 

time: 852 us -> 793 us (0.931)
  local copies, waits for them, and re-layouts: 109 us -> 54.6 us
    while x31, local copies, waits for them, and re-layouts: 29 us -> 1.94 us
    all_to_all x2 -> x0, local copies, waits for them, and re-layouts: 18.2 us -> none  [shards(): lax.all_to_all(masked, 'row', split_axis=0, concat_axis=2, tiled=True)]
    unnamed x7 -> x36, local copies, waits for them, and re-layouts: 51.1 us -> 49 us
where the time goes in v1:
time: 793 us
  starting transfers between devices  404 us (51%)
  waiting for transfers between devices  272 us (34%)
  local copies, waits for them, and re-layouts  54.6 us (7%)
  matrix products  46.5 us (6%)
  between operations  13.5 us (2%)
    ppermute x31, starting transfers between devices, shifted(): return lax.ppermute(block, axis, route)  395 us
    unnamed x2, waiting for transfers between devices  152 us
    ppermute x31, waiting for transfers between devices, shifted(): return lax.ppermute(block, axis, route)  102 us
    unnamed x36, local copies, waits for them, and re-layouts  49 us
    dot_general x32, matrix products, tile_with(): lax.dot_general(own_rows, visitor, (((1,), (1,)), ((), ())), preferred_el...  46.5 us
    all_to_all x1, waiting for transfers between devices, map_refer(): lax.all_to_all(jnp.stack(jnp.split(xin, lax.axis_size('row'), axis=0), ax...  18.3 us
  transfers between devices with their start and end apart: 33, of which 33 were waited for; matrix products, arithmetic and copies ran while one was open for 0% of the time, Pallas kernels for 0%

profile of v1, /device:TPU:1, one launch (start us, length us, event | category | flops | bytes accessed | tf_op | source)
XLA Modules:
  0.0 792.7 jit_solution(7806280949627677660)
XLA Ops:
  41.4 18.3 %all-to-all-done = bf16[32,312,2,24]{1,3,2,0:T(8,128)(2,1)S(1)} async-done(((bf16[32,312,2,24]{1,3,2,0:T(8,128)(2,1)}), bf16[32,312,2,24]{1,3,2,0:T(8,128)(2,1)S(1)}, u32[]{:S(2)}, u32[]{:S(2)}) %all-to-all-start) | async-done | bytes 958496 | tf_op jit(solution)/shard_map/all_to_all | solution.py:9
  67.7 544.2 %while.17 = (s32[]{:T(128)}, bf16[312,1536]{1,0:T(8,128)(2,1)S(1)}, f32[312,32,312]{2,0,1:T(8,128)}, bf16[312,1536]{1,0:T(8,128)(2,1)S(1)}, s32[]{:T(128)}, /*index=5*/s32[]{:T(128)}, s32[]{:T(128)}, s32[]{:T(128)}, s32[]{:T(128)}) while((s32[]{:T(128)}, bf16[312,1536]{1,0:T(8,128)(2,1)S(1)}, f32[312,32,312]{2,0,1:T(8,128)}, ...), condition=%wide.region_1.2_spmd, body=%wide.region_0.1_spmd.sunk | while | flops 299040768 | bytes 8147236 | solution.py:50
  67.8 13.1 %collective-permute-done = bf16[312,1536]{1,0:T(8,128)(2,1)S(1)} collective-permute-done((bf16[312,1536]{1,0:T(8,128)(2,1)S(1)}, bf16[312,1536]{1,0:T(8,128)(2,1)S(1)}, u32[]{:S(2)}, u32[]{:S(2)}) %collective-permute-start) | collective-permute-done | bytes 958496 | tf_op jit(solution)/shard_map/while/body/eval_jaxpr/ppermute | solution.py:20
  82.6 13.1 %collective-permute-done = bf16[312,1536]{1,0:T(8,128)(2,1)S(1)} collective-permute-done((bf16[312,1536]{1,0:T(8,128)(2,1)S(1)}, bf16[312,1536]{1,0:T(8,128)(2,1)S(1)}, u32[]{:S(2)}, u32[]{:S(2)}) %collective-permute-start) | collective-permute-done | bytes 958496 | tf_op jit(solution)/shard_map/while/body/eval_jaxpr/ppermute | solution.py:20
  141.6 13.4 %collective-permute-start = (bf16[312,1536]{1,0:T(8,128)(2,1)S(1)}, bf16[312,1536]{1,0:T(8,128)(2,1)S(1)}, u32[]{:S(2)}, u32[]{:S(2)}) collective-permute-start(bf16[312,1536]{1,0:T(8,128)(2,1)S(1)} %get-tuple-element.350), channel_id=1, source_target_pairs={{1,0},{2,1},{3,2},{4,3},{5,4},{6,5},{7,6},{8,7},{9,8},{10,9},{11,1... | collective-permute-start | bytes 2875400 | tf_op jit(solution)/shard_map/while/body/eval_jaxpr/ppermute | solution.py:20
  158.8 14.5 %collective-permute-start = (bf16[312,1536]{1,0:T(8,128)(2,1)S(1)}, bf16[312,1536]{1,0:T(8,128)(2,1)S(1)}, u32[]{:S(2)}, u32[]{:S(2)}) collective-permute-start(bf16[312,1536]{1,0:T(8,128)(2,1)S(1)} %get-tuple-element.350), channel_id=1, source_target_pairs={{1,0},{2,1},{3,2},{4,3},{5,4},{6,5},{7,6},{8,7},{9,8},{10,9},{11,1... | collective-permute-start | bytes 2875400 | tf_op jit(solution)/shard_map/while/body/eval_jaxpr/ppermute | solution.py:20
  176.9 14.4 %collective-permute-start = (bf16[312,1536]{1,0:T(8,128)(2,1)S(1)}, bf16[312,1536]{1,0:T(8,128)(2,1)S(1)}, u32[]{:S(2)}, u32[]{:S(2)}) collective-permute-start(bf16[312,1536]{1,0:T(8,128)(2,1)S(1)} %get-tuple-element.350), channel_id=1, source_target_pairs={{1,0},{2,1},{3,2},{4,3},{5,4},{6,5},{7,6},{8,7},{9,8},{10,9},{11,1... | collective-permute-start | bytes 2875400 | tf_op jit(solution)/shard_map/while/body/eval_jaxpr/ppermute | solution.py:20
  195.0 14.4 %collective-permute-start = (bf16[312,1536]{1,0:T(8,128)(2,1)S(1)}, bf16[312,1536]{1,0:T(8,128)(2,1)S(1)}, u32[]{:S(2)}, u32[]{:S(2)}) collective-permute-start(bf16[312,1536]{1,0:T(8,128)(2,1)S(1)} %get-tuple-element.350), channel_id=1, source_target_pairs={{1,0},{2,1},{3,2},{4,3},{5,4},{6,5},{7,6},{8,7},{9,8},{10,9},{11,1... | collective-permute-start | bytes 2875400 | tf_op jit(solution)/shard_map/while/body/eval_jaxpr/ppermute | solution.py:20
  213.1 14.4 %collective-permute-start = (bf16[312,1536]{1,0:T(8,128)(2,1)S(1)}, bf16[312,1536]{1,0:T(8,128)(2,1)S(1)}, u32[]{:S(2)}, u32[]{:S(2)}) collective-permute-start(bf16[312,1536]{1,0:T(8,128)(2,1)S(1)} %get-tuple-element.350), channel_id=1, source_target_pairs={{1,0},{2,1},{3,2},{4,3},{5,4},{6,5},{7,6},{8,7},{9,8},{10,9},{11,1... | collective-permute-start | bytes 2875400 | tf_op jit(solution)/shard_map/while/body/eval_jaxpr/ppermute | solution.py:20
  231.3 14.4 %collective-permute-start = (bf16[312,1536]{1,0:T(8,128)(2,1)S(1)}, bf16[312,1536]{1,0:T(8,128)(2,1)S(1)}, u32[]{:S(2)}, u32[]{:S(2)}) collective-permute-start(bf16[312,1536]{1,0:T(8,128)(2,1)S(1)} %get-tuple-element.350), channel_id=1, source_target_pairs={{1,0},{2,1},{3,2},{4,3},{5,4},{6,5},{7,6},{8,7},{9,8},{10,9},{11,1... | collective-permute-start | bytes 2875400 | tf_op jit(solution)/shard_map/while/body/eval_jaxpr/ppermute | solution.py:20
  249.3 14.5 %collective-permute-start = (bf16[312,1536]{1,0:T(8,128)(2,1)S(1)}, bf16[312,1536]{1,0:T(8,128)(2,1)S(1)}, u32[]{:S(2)}, u32[]{:S(2)}) collective-permute-start(bf16[312,1536]{1,0:T(8,128)(2,1)S(1)} %get-tuple-element.350), channel_id=1, source_target_pairs={{1,0},{2,1},{3,2},{4,3},{5,4},{6,5},{7,6},{8,7},{9,8},{10,9},{11,1... | collective-permute-start | bytes 2875400 | tf_op jit(solution)/shard_map/while/body/eval_jaxpr/ppermute | solution.py:20
  267.5 14.4 %collective-permute-start = (bf16[312,1536]{1,0:T(8,128)(2,1)S(1)}, bf16[312,1536]{1,0:T(8,128)(2,1)S(1)}, u32[]{:S(2)}, u32[]{:S(2)}) collective-permute-start(bf16[312,1536]{1,0:T(8,128)(2,1)S(1)} %get-tuple-element.350), channel_id=1, source_target_pairs={{1,0},{2,1},{3,2},{4,3},{5,4},{6,5},{7,6},{8,7},{9,8},{10,9},{11,1... | collective-permute-start | bytes 2875400 | tf_op jit(solution)/shard_map/while/body/eval_jaxpr/ppermute | solution.py:20
  285.6 14.4 %collective-permute-start = (bf16[312,1536]{1,0:T(8,128)(2,1)S(1)}, bf16[312,1536]{1,0:T(8,128)(2,1)S(1)}, u32[]{:S(2)}, u32[]{:S(2)}) collective-permute-start(bf16[312,1536]{1,0:T(8,128)(2,1)S(1)} %get-tuple-element.350), channel_id=1, source_target_pairs={{1,0},{2,1},{3,2},{4,3},{5,4},{6,5},{7,6},{8,7},{9,8},{10,9},{11,1... | collective-permute-start | bytes 2875400 | tf_op jit(solution)/shard_map/while/body/eval_jaxpr/ppermute | solution.py:20
  303.7 14.4 %collective-permute-start = (bf16[312,1536]{1,0:T(8,128)(2,1)S(1)}, bf16[312,1536]{1,0:T(8,128)(2,1)S(1)}, u32[]{:S(2)}, u32[]{:S(2)}) collective-permute-start(bf16[312,1536]{1,0:T(8,128)(2,1)S(1)} %get-tuple-element.350), channel_id=1, source_target_pairs={{1,0},{2,1},{3,2},{4,3},{5,4},{6,5},{7,6},{8,7},{9,8},{10,9},{11,1... | collective-permute-start | bytes 2875400 | tf_op jit(solution)/shard_map/while/body/eval_jaxpr/ppermute | solution.py:20
  321.8 14.4 %collective-permute-start = (bf16[312,1536]{1,0:T(8,128)(2,1)S(1)}, bf16[312,1536]{1,0:T(8,128)(2,1)S(1)}, u32[]{:S(2)}, u32[]{:S(2)}) collective-permute-start(bf16[312,1536]{1,0:T(8,128)(2,1)S(1)} %get-tuple-element.350), channel_id=1, source_target_pairs={{1,0},{2,1},{3,2},{4,3},{5,4},{6,5},{7,6},{8,7},{9,8},{10,9},{11,1... | collective-permute-start | bytes 2875400 | tf_op jit(solution)/shard_map/while/body/eval_jaxpr/ppermute | solution.py:20
  340.0 14.4 %collective-permute-start = (bf16[312,1536]{1,0:T(8,128)(2,1)S(1)}, bf16[312,1536]{1,0:T(8,128)(2,1)S(1)}, u32[]{:S(2)}, u32[]{:S(2)}) collective-permute-start(bf16[312,1536]{1,0:T(8,128)(2,1)S(1)} %get-tuple-element.350), channel_id=1, source_target_pairs={{1,0},{2,1},{3,2},{4,3},{5,4},{6,5},{7,6},{8,7},{9,8},{10,9},{11,1... | collective-permute-start | bytes 2875400 | tf_op jit(solution)/shard_map/while/body/eval_jaxpr/ppermute | solution.py:20
  358.1 14.4 %collective-permute-start = (bf16[312,1536]{1,0:T(8,128)(2,1)S(1)}, bf16[312,1536]{1,0:T(8,128)(2,1)S(1)}, u32[]{:S(2)}, u32[]{:S(2)}) collective-permute-start(bf16[312,1536]{1,0:T(8,128)(2,1)S(1)} %get-tuple-element.350), channel_id=1, source_target_pairs={{1,0},{2,1},{3,2},{4,3},{5,4},{6,5},{7,6},{8,7},{9,8},{10,9},{11,1... | collective-permute-start | bytes 2875400 | tf_op jit(solution)/shard_map/while/body/eval_jaxpr/ppermute | solution.py:20
  376.3 14.4 %collective-permute-start = (bf16[312,1536]{1,0:T(8,128)(2,1)S(1)}, bf16[312,1536]{1,0:T(8,128)(2,1)S(1)}, u32[]{:S(2)}, u32[]{:S(2)}) collective-permute-start(bf16[312,1536]{1,0:T(8,128)(2,1)S(1)} %get-tuple-element.350), channel_id=1, source_target_pairs={{1,0},{2,1},{3,2},{4,3},{5,4},{6,5},{7,6},{8,7},{9,8},{10,9},{11,1... | collective-permute-start | bytes 2875400 | tf_op jit(solution)/shard_map/while/body/eval_jaxpr/ppermute | solution.py:20
  394.4 14.4 %collective-permute-start = (bf16[312,1536]{1,0:T(8,128)(2,1)S(1)}, bf16[312,1536]{1,0:T(8,128)(2,1)S(1)}, u32[]{:S(2)}, u32[]{:S(2)}) collective-permute-start(bf16[312,1536]{1,0:T(8,128)(2,1)S(1)} %get-tuple-element.350), channel_id=1, source_target_pairs={{1,0},{2,1},{3,2},{4,3},{5,4},{6,5},{7,6},{8,7},{9,8},{10,9},{11,1... | collective-permute-start | bytes 2875400 | tf_op jit(solution)/shard_map/while/body/eval_jaxpr/ppermute | solution.py:20
  412.5 14.5 %collective-permute-start = (bf16[312,1536]{1,0:T(8,128)(2,1)S(1)}, bf16[312,1536]{1,0:T(8,128)(2,1)S(1)}, u32[]{:S(2)}, u32[]{:S(2)}) collective-permute-start(bf16[312,1536]{1,0:T(8,128)(2,1)S(1)} %get-tuple-element.350), channel_id=1, source_target_pairs={{1,0},{2,1},{3,2},{4,3},{5,4},{6,5},{7,6},{8,7},{9,8},{10,9},{11,1... | collective-permute-start | bytes 2875400 | tf_op jit(solution)/shard_map/while/body/eval_jaxpr/ppermute | solution.py:20
  430.7 14.4 %collective-permute-start = (bf16[312,1536]{1,0:T(8,128)(2,1)S(1)}, bf16[312,1536]{1,0:T(8,128)(2,1)S(1)}, u32[]{:S(2)}, u32[]{:S(2)}) collective-permute-start(bf16[312,1536]{1,0:T(8,128)(2,1)S(1)} %get-tuple-element.350), channel_id=1, source_target_pairs={{1,0},{2,1},{3,2},{4,3},{5,4},{6,5},{7,6},{8,7},{9,8},{10,9},{11,1... | collective-permute-start | bytes 2875400 | tf_op jit(solution)/shard_map/while/body/eval_jaxpr/ppermute | solution.py:20
  448.8 14.5 %collective-permute-start = (bf16[312,1536]{1,0:T(8,128)(2,1)S(1)}, bf16[312,1536]{1,0:T(8,128)(2,1)S(1)}, u32[]{:S(2)}, u32[]{:S(2)}) collective-permute-start(bf16[312,1536]{1,0:T(8,128)(2,1)S(1)} %get-tuple-element.350), channel_id=1, source_target_pairs={{1,0},{2,1},{3,2},{4,3},{5,4},{6,5},{7,6},{8,7},{9,8},{10,9},{11,1... | collective-permute-start | bytes 2875400 | tf_op jit(solution)/shard_map/while/body/eval_jaxpr/ppermute | solution.py:20
  466.9 14.4 %collective-permute-start = (bf16[312,1536]{1,0:T(8,128)(2,1)S(1)}, bf16[312,1536]{1,0:T(8,128)(2,1)S(1)}, u32[]{:S(2)}, u32[]{:S(2)}) collective-permute-start(bf16[312,1536]{1,0:T(8,128)(2,1)S(1)} %get-tuple-element.350), channel_id=1, source_target_pairs={{1,0},{2,1},{3,2},{4,3},{5,4},{6,5},{7,6},{8,7},{9,8},{10,9},{11,1... | collective-permute-start | bytes 2875400 | tf_op jit(solution)/shard_map/while/body/eval_jaxpr/ppermute | solution.py:20
  485.0 14.4 %collective-permute-start = (bf16[312,1536]{1,0:T(8,128)(2,1)S(1)}, bf16[312,1536]{1,0:T(8,128)(2,1)S(1)}, u32[]{:S(2)}, u32[]{:S(2)}) collective-permute-start(bf16[312,1536]{1,0:T(8,128)(2,1)S(1)} %get-tuple-element.350), channel_id=1, source_target_pairs={{1,0},{2,1},{3,2},{4,3},{5,4},{6,5},{7,6},{8,7},{9,8},{10,9},{11,1... | collective-permute-start | bytes 2875400 | tf_op jit(solution)/shard_map/while/body/eval_jaxpr/ppermute | solution.py:20
  503.1 14.4 %collective-permute-start = (bf16[312,1536]{1,0:T(8,128)(2,1)S(1)}, bf16[312,1536]{1,0:T(8,128)(2,1)S(1)}, u32[]{:S(2)}, u32[]{:S(2)}) collective-permute-start(bf16[312,1536]{1,0:T(8,128)(2,1)S(1)} %get-tuple-element.350), channel_id=1, source_target_pairs={{1,0},{2,1},{3,2},{4,3},{5,4},{6,5},{7,6},{8,7},{9,8},{10,9},{11,1... | collective-permute-start | bytes 2875400 | tf_op jit(solution)/shard_map/while/body/eval_jaxpr/ppermute | solution.py:20
  521.3 14.4 %collective-permute-start = (bf16[312,1536]{1,0:T(8,128)(2,1)S(1)}, bf16[312,1536]{1,0:T(8,128)(2,1)S(1)}, u32[]{:S(2)}, u32[]{:S(2)}) collective-permute-start(bf16[312,1536]{1,0:T(8,128)(2,1)S(1)} %get-tuple-element.350), channel_id=1, source_target_pairs={{1,0},{2,1},{3,2},{4,3},{5,4},{6,5},{7,6},{8,7},{9,8},{10,9},{11,1... | collective-permute-start | bytes 2875400 | tf_op jit(solution)/shard_map/while/body/eval_jaxpr/ppermute | solution.py:20
  539.4 14.5 %collective-permute-start = (bf16[312,1536]{1,0:T(8,128)(2,1)S(1)}, bf16[312,1536]{1,0:T(8,128)(2,1)S(1)}, u32[]{:S(2)}, u32[]{:S(2)}) collective-permute-start(bf16[312,1536]{1,0:T(8,128)(2,1)S(1)} %get-tuple-element.350), channel_id=1, source_target_pairs={{1,0},{2,1},{3,2},{4,3},{5,4},{6,5},{7,6},{8,7},{9,8},{10,9},{11,1... | collective-permute-start | bytes 2875400 | tf_op jit(solution)/shard_map/while/body/eval_jaxpr/ppermute | solution.py:20
  557.6 14.4 %collective-permute-start = (bf16[312,1536]{1,0:T(8,128)(2,1)S(1)}, bf16[312,1536]{1,0:T(8,128)(2,1)S(1)}, u32[]{:S(2)}, u32[]{:S(2)}) collective-permute-start(bf16[312,1536]{1,0:T(8,128)(2,1)S(1)} %get-tuple-element.350), channel_id=1, source_target_pairs={{1,0},{2,1},{3,2},{4,3},{5,4},{6,5},{7,6},{8,7},{9,8},{10,9},{11,1... | collective-permute-start | bytes 2875400 | tf_op jit(solution)/shard_map/while/body/eval_jaxpr/ppermute | solution.py:20
  575.6 14.5 %collective-permute-start = (bf16[312,1536]{1,0:T(8,128)(2,1)S(1)}, bf16[312,1536]{1,0:T(8,128)(2,1)S(1)}, u32[]{:S(2)}, u32[]{:S(2)}) collective-permute-start(bf16[312,1536]{1,0:T(8,128)(2,1)S(1)} %get-tuple-element.350), channel_id=1, source_target_pairs={{1,0},{2,1},{3,2},{4,3},{5,4},{6,5},{7,6},{8,7},{9,8},{10,9},{11,1... | collective-permute-start | bytes 2875400 | tf_op jit(solution)/shard_map/while/body/eval_jaxpr/ppermute | solution.py:20
  593.8 14.4 %collective-permute-start = (bf16[312,1536]{1,0:T(8,128)(2,1)S(1)}, bf16[312,1536]{1,0:T(8,128)(2,1)S(1)}, u32[]{:S(2)}, u32[]{:S(2)}) collective-permute-start(bf16[312,1536]{1,0:T(8,128)(2,1)S(1)} %get-tuple-element.350), channel_id=1, source_target_pairs={{1,0},{2,1},{3,2},{4,3},{5,4},{6,5},{7,6},{8,7},{9,8},{10,9},{11,1... | collective-permute-start | bytes 2875400 | tf_op jit(solution)/shard_map/while/body/eval_jaxpr/ppermute | solution.py:20
  611.9 16.9 %copy.1130 = f32[312,32,312]{0,2,1:T(8,128)} copy(f32[312,32,312]{2,0,1:T(8,128)} %get-tuple-element.138) | data formatting | bytes 24920064
  628.9 151.8 %reduce-scatter.4.cloned.1.call-done = f32[2496,312]{1,0:T(8,128)} async-done(((f32[9984,312]{1,0:T(8,128)}), f32[2496,312]{1,0:T(8,128)}) %reduce-scatter.4.cloned.1.call-update) | async-done | bytes 3115024
  (142 shorter events, 191.7 us)
Async XLA Ops:
  32.0 27.8 %all-to-all-start = ((bf16[32,312,2,24]{1,3,2,0:T(8,128)(2,1)}), bf16[32,312,2,24]{1,3,2,0:T(8,128)(2,1)S(1)}, u32[]{:S(2)}, u32[]{:S(2)}) async-start(bf16[32,312,2,24]{1,3,2,0:T(8,128)(2,1)} %constant_dynamic-update-slice_fusion), calls=%async_computation | async-start | bytes 2359296 | tf_op jit(solution)/shard_map/all_to_all | solution.py:9
  41.4 739.3 %reduce-scatter.4.cloned.1.call-start = ((), (), s32[]{:S(2)}) async-start(), calls=%async_computation.2 | async-start | bytes 19169280
  67.7 13.3 %collective-permute-start = (bf16[312,1536]{1,0:T(8,128)(2,1)S(1)}, bf16[312,1536]{1,0:T(8,128)(2,1)S(1)}, u32[]{:S(2)}, u32[]{:S(2)}) collective-permute-start(bf16[312,1536]{1,0:T(8,128)(2,1)S(1)} %get-tuple-element.350), channel_id=1, source_target_pairs={{1,0},{2,1},{3,2},{4,3},{5,4},{6,5},{7,6},{8,7},{9,8},{10,9},{11,1... | collective-permute-start | bytes 2875400 | tf_op jit(solution)/shard_map/while/body/eval_jaxpr/ppermute | solution.py:20
  82.5 13.3 %collective-permute-start = (bf16[312,1536]{1,0:T(8,128)(2,1)S(1)}, bf16[312,1536]{1,0:T(8,128)(2,1)S(1)}, u32[]{:S(2)}, u32[]{:S(2)}) collective-permute-start(bf16[312,1536]{1,0:T(8,128)(2,1)S(1)} %get-tuple-element.350), channel_id=1, source_target_pairs={{1,0},{2,1},{3,2},{4,3},{5,4},{6,5},{7,6},{8,7},{9,8},{10,9},{11,1... | collective-permute-start | bytes 2875400 | tf_op jit(solution)/shard_map/while/body/eval_jaxpr/ppermute | solution.py:20
  97.3 13.3 %collective-permute-start = (bf16[312,1536]{1,0:T(8,128)(2,1)S(1)}, bf16[312,1536]{1,0:T(8,128)(2,1)S(1)}, u32[]{:S(2)}, u32[]{:S(2)}) collective-permute-start(bf16[312,1536]{1,0:T(8,128)(2,1)S(1)} %get-tuple-element.350), channel_id=1, source_target_pairs={{1,0},{2,1},{3,2},{4,3},{5,4},{6,5},{7,6},{8,7},{9,8},{10,9},{11,1... | collective-permute-start | bytes 2875400 | tf_op jit(solution)/shard_map/while/body/eval_jaxpr/ppermute | solution.py:20
  112.1 13.3 %collective-permute-start = (bf16[312,1536]{1,0:T(8,128)(2,1)S(1)}, bf16[312,1536]{1,0:T(8,128)(2,1)S(1)}, u32[]{:S(2)}, u32[]{:S(2)}) collective-permute-start(bf16[312,1536]{1,0:T(8,128)(2,1)S(1)} %get-tuple-element.350), channel_id=1, source_target_pairs={{1,0},{2,1},{3,2},{4,3},{5,4},{6,5},{7,6},{8,7},{9,8},{10,9},{11,1... | collective-permute-start | bytes 2875400 | tf_op jit(solution)/shard_map/while/body/eval_jaxpr/ppermute | solution.py:20
  141.6 15.6 %collective-permute-start = (bf16[312,1536]{1,0:T(8,128)(2,1)S(1)}, bf16[312,1536]{1,0:T(8,128)(2,1)S(1)}, u32[]{:S(2)}, u32[]{:S(2)}) collective-permute-start(bf16[312,1536]{1,0:T(8,128)(2,1)S(1)} %get-tuple-element.350), channel_id=1, source_target_pairs={{1,0},{2,1},{3,2},{4,3},{5,4},{6,5},{7,6},{8,7},{9,8},{10,9},{11,1... | collective-permute-start | bytes 2875400 | tf_op jit(solution)/shard_map/while/body/eval_jaxpr/ppermute | solution.py:20
  158.8 16.6 %collective-permute-start = (bf16[312,1536]{1,0:T(8,128)(2,1)S(1)}, bf16[312,1536]{1,0:T(8,128)(2,1)S(1)}, u32[]{:S(2)}, u32[]{:S(2)}) collective-permute-start(bf16[312,1536]{1,0:T(8,128)(2,1)S(1)} %get-tuple-element.350), channel_id=1, source_target_pairs={{1,0},{2,1},{3,2},{4,3},{5,4},{6,5},{7,6},{8,7},{9,8},{10,9},{11,1... | collective-permute-start | bytes 2875400 | tf_op jit(solution)/shard_map/while/body/eval_jaxpr/ppermute | solution.py:20
  176.9 16.6 %collective-permute-start = (bf16[312,1536]{1,0:T(8,128)(2,1)S(1)}, bf16[312,1536]{1,0:T(8,128)(2,1)S(1)}, u32[]{:S(2)}, u32[]{:S(2)}) collective-permute-start(bf16[312,1536]{1,0:T(8,128)(2,1)S(1)} %get-tuple-element.350), channel_id=1, source_target_pairs={{1,0},{2,1},{3,2},{4,3},{5,4},{6,5},{7,6},{8,7},{9,8},{10,9},{11,1... | collective-permute-start | bytes 2875400 | tf_op jit(solution)/shard_map/while/body/eval_jaxpr/ppermute | solution.py:20
  195.0 16.6 %collective-permute-start = (bf16[312,1536]{1,0:T(8,128)(2,1)S(1)}, bf16[312,1536]{1,0:T(8,128)(2,1)S(1)}, u32[]{:S(2)}, u32[]{:S(2)}) collective-permute-start(bf16[312,1536]{1,0:T(8,128)(2,1)S(1)} %get-tuple-element.350), channel_id=1, source_target_pairs={{1,0},{2,1},{3,2},{4,3},{5,4},{6,5},{7,6},{8,7},{9,8},{10,9},{11,1... | collective-permute-start | bytes 2875400 | tf_op jit(solution)/shard_map/while/body/eval_jaxpr/ppermute | solution.py:20
  213.1 16.6 %collective-permute-start = (bf16[312,1536]{1,0:T(8,128)(2,1)S(1)}, bf16[312,1536]{1,0:T(8,128)(2,1)S(1)}, u32[]{:S(2)}, u32[]{:S(2)}) collective-permute-start(bf16[312,1536]{1,0:T(8,128)(2,1)S(1)} %get-tuple-element.350), channel_id=1, source_target_pairs={{1,0},{2,1},{3,2},{4,3},{5,4},{6,5},{7,6},{8,7},{9,8},{10,9},{11,1... | collective-permute-start | bytes 2875400 | tf_op jit(solution)/shard_map/while/body/eval_jaxpr/ppermute | solution.py:20
  231.3 16.5 %collective-permute-start = (bf16[312,1536]{1,0:T(8,128)(2,1)S(1)}, bf16[312,1536]{1,0:T(8,128)(2,1)S(1)}, u32[]{:S(2)}, u32[]{:S(2)}) collective-permute-start(bf16[312,1536]{1,0:T(8,128)(2,1)S(1)} %get-tuple-element.350), channel_id=1, source_target_pairs={{1,0},{2,1},{3,2},{4,3},{5,4},{6,5},{7,6},{8,7},{9,8},{10,9},{11,1... | collective-permute-start | bytes 2875400 | tf_op jit(solution)/shard_map/while/body/eval_jaxpr/ppermute | solution.py:20
  249.3 16.6 %collective-permute-start = (bf16[312,1536]{1,0:T(8,128)(2,1)S(1)}, bf16[312,1536]{1,0:T(8,128)(2,1)S(1)}, u32[]{:S(2)}, u32[]{:S(2)}) collective-permute-start(bf16[312,1536]{1,0:T(8,128)(2,1)S(1)} %get-tuple-element.350), channel_id=1, source_target_pairs={{1,0},{2,1},{3,2},{4,3},{5,4},{6,5},{7,6},{8,7},{9,8},{10,9},{11,1... | collective-permute-start | bytes 2875400 | tf_op jit(solution)/shard_map/while/body/eval_jaxpr/ppermute | solution.py:20
  267.5 16.5 %collective-permute-start = (bf16[312,1536]{1,0:T(8,128)(2,1)S(1)}, bf16[312,1536]{1,0:T(8,128)(2,1)S(1)}, u32[]{:S(2)}, u32[]{:S(2)}) collective-permute-start(bf16[312,1536]{1,0:T(8,128)(2,1)S(1)} %get-tuple-element.350), channel_id=1, source_target_pairs={{1,0},{2,1},{3,2},{4,3},{5,4},{6,5},{7,6},{8,7},{9,8},{10,9},{11,1... | collective-permute-start | bytes 2875400 | tf_op jit(solution)/shard_map/while/body/eval_jaxpr/ppermute | solution.py:20
  285.6 16.6 %collective-permute-start = (bf16[312,1536]{1,0:T(8,128)(2,1)S(1)}, bf16[312,1536]{1,0:T(8,128)(2,1)S(1)}, u32[]{:S(2)}, u32[]{:S(2)}) collective-permute-start(bf16[312,1536]{1,0:T(8,128)(2,1)S(1)} %get-tuple-element.350), channel_id=1, source_target_pairs={{1,0},{2,1},{3,2},{4,3},{5,4},{6,5},{7,6},{8,7},{9,8},{10,9},{11,1... | collective-permute-start | bytes 2875400 | tf_op jit(solution)/shard_map/while/body/eval_jaxpr/ppermute | solution.py:20
  303.7 16.6 %collective-permute-start = (bf16[312,1536]{1,0:T(8,128)(2,1)S(1)}, bf16[312,1536]{1,0:T(8,128)(2,1)S(1)}, u32[]{:S(2)}, u32[]{:S(2)}) collective-permute-start(bf16[312,1536]{1,0:T(8,128)(2,1)S(1)} %get-tuple-element.350), channel_id=1, source_target_pairs={{1,0},{2,1},{3,2},{4,3},{5,4},{6,5},{7,6},{8,7},{9,8},{10,9},{11,1... | collective-permute-start | bytes 2875400 | tf_op jit(solution)/shard_map/while/body/eval_jaxpr/ppermute | solution.py:20
  321.8 16.6 %collective-permute-start = (bf16[312,1536]{1,0:T(8,128)(2,1)S(1)}, bf16[312,1536]{1,0:T(8,128)(2,1)S(1)}, u32[]{:S(2)}, u32[]{:S(2)}) collective-permute-start(bf16[312,1536]{1,0:T(8,128)(2,1)S(1)} %get-tuple-element.350), channel_id=1, source_target_pairs={{1,0},{2,1},{3,2},{4,3},{5,4},{6,5},{7,6},{8,7},{9,8},{10,9},{11,1... | collective-permute-start | bytes 2875400 | tf_op jit(solution)/shard_map/while/body/eval_jaxpr/ppermute | solution.py:20
  340.0 16.5 %collective-permute-start = (bf16[312,1536]{1,0:T(8,128)(2,1)S(1)}, bf16[312,1536]{1,0:T(8,128)(2,1)S(1)}, u32[]{:S(2)}, u32[]{:S(2)}) collective-permute-start(bf16[312,1536]{1,0:T(8,128)(2,1)S(1)} %get-tuple-element.350), channel_id=1, source_target_pairs={{1,0},{2,1},{3,2},{4,3},{5,4},{6,5},{7,6},{8,7},{9,8},{10,9},{11,1... | collective-permute-start | bytes 2875400 | tf_op jit(solution)/shard_map/while/body/eval_jaxpr/ppermute | solution.py:20
  358.1 16.6 %collective-permute-start = (bf16[312,1536]{1,0:T(8,128)(2,1)S(1)}, bf16[312,1536]{1,0:T(8,128)(2,1)S(1)}, u32[]{:S(2)}, u32[]{:S(2)}) collective-permute-start(bf16[312,1536]{1,0:T(8,128)(2,1)S(1)} %get-tuple-element.350), channel_id=1, source_target_pairs={{1,0},{2,1},{3,2},{4,3},{5,4},{6,5},{7,6},{8,7},{9,8},{10,9},{11,1... | collective-permute-start | bytes 2875400 | tf_op jit(solution)/shard_map/while/body/eval_jaxpr/ppermute | solution.py:20
  376.3 16.5 %collective-permute-start = (bf16[312,1536]{1,0:T(8,128)(2,1)S(1)}, bf16[312,1536]{1,0:T(8,128)(2,1)S(1)}, u32[]{:S(2)}, u32[]{:S(2)}) collective-permute-start(bf16[312,1536]{1,0:T(8,128)(2,1)S(1)} %get-tuple-element.350), channel_id=1, source_target_pairs={{1,0},{2,1},{3,2},{4,3},{5,4},{6,5},{7,6},{8,7},{9,8},{10,9},{11,1... | collective-permute-start | bytes 2875400 | tf_op jit(solution)/shard_map/while/body/eval_jaxpr/ppermute | solution.py:20
  394.4 16.6 %collective-permute-start = (bf16[312,1536]{1,0:T(8,128)(2,1)S(1)}, bf16[312,1536]{1,0:T(8,128)(2,1)S(1)}, u32[]{:S(2)}, u32[]{:S(2)}) collective-permute-start(bf16[312,1536]{1,0:T(8,128)(2,1)S(1)} %get-tuple-element.350), channel_id=1, source_target_pairs={{1,0},{2,1},{3,2},{4,3},{5,4},{6,5},{7,6},{8,7},{9,8},{10,9},{11,1... | collective-permute-start | bytes 2875400 | tf_op jit(solution)/shard_map/while/body/eval_jaxpr/ppermute | solution.py:20
  412.5 16.6 %collective-permute-start = (bf16[312,1536]{1,0:T(8,128)(2,1)S(1)}, bf16[312,1536]{1,0:T(8,128)(2,1)S(1)}, u32[]{:S(2)}, u32[]{:S(2)}) collective-permute-start(bf16[312,1536]{1,0:T(8,128)(2,1)S(1)} %get-tuple-element.350), channel_id=1, source_target_pairs={{1,0},{2,1},{3,2},{4,3},{5,4},{6,5},{7,6},{8,7},{9,8},{10,9},{11,1... | collective-permute-start | bytes 2875400 | tf_op jit(solution)/shard_map/while/body/eval_jaxpr/ppermute | solution.py:20
  430.7 16.6 %collective-permute-start = (bf16[312,1536]{1,0:T(8,128)(2,1)S(1)}, bf16[312,1536]{1,0:T(8,128)(2,1)S(1)}, u32[]{:S(2)}, u32[]{:S(2)}) collective-permute-start(bf16[312,1536]{1,0:T(8,128)(2,1)S(1)} %get-tuple-element.350), channel_id=1, source_target_pairs={{1,0},{2,1},{3,2},{4,3},{5,4},{6,5},{7,6},{8,7},{9,8},{10,9},{11,1... | collective-permute-start | bytes 2875400 | tf_op jit(solution)/shard_map/while/body/eval_jaxpr/ppermute | solution.py:20
  448.8 16.6 %collective-permute-start = (bf16[312,1536]{1,0:T(8,128)(2,1)S(1)}, bf16[312,1536]{1,0:T(8,128)(2,1)S(1)}, u32[]{:S(2)}, u32[]{:S(2)}) collective-permute-start(bf16[312,1536]{1,0:T(8,128)(2,1)S(1)} %get-tuple-element.350), channel_id=1, source_target_pairs={{1,0},{2,1},{3,2},{4,3},{5,4},{6,5},{7,6},{8,7},{9,8},{10,9},{11,1... | collective-permute-start | bytes 2875400 | tf_op jit(solution)/shard_map/while/body/eval_jaxpr/ppermute | solution.py:20
  466.9 16.6 %collective-permute-start = (bf16[312,1536]{1,0:T(8,128)(2,1)S(1)}, bf16[312,1536]{1,0:T(8,128)(2,1)S(1)}, u32[]{:S(2)}, u32[]{:S(2)}) collective-permute-start(bf16[312,1536]{1,0:T(8,128)(2,1)S(1)} %get-tuple-element.350), channel_id=1, source_target_pairs={{1,0},{2,1},{3,2},{4,3},{5,4},{6,5},{7,6},{8,7},{9,8},{10,9},{11,1... | collective-permute-start | bytes 2875400 | tf_op jit(solution)/shard_map/while/body/eval_jaxpr/ppermute | solution.py:20
  485.0 16.6 %collective-permute-start = (bf16[312,1536]{1,0:T(8,128)(2,1)S(1)}, bf16[312,1536]{1,0:T(8,128)(2,1)S(1)}, u32[]{:S(2)}, u32[]{:S(2)}) collective-permute-start(bf16[312,1536]{1,0:T(8,128)(2,1)S(1)} %get-tuple-element.350), channel_id=1, source_target_pairs={{1,0},{2,1},{3,2},{4,3},{5,4},{6,5},{7,6},{8,7},{9,8},{10,9},{11,1... | collective-permute-start | bytes 2875400 | tf_op jit(solution)/shard_map/while/body/eval_jaxpr/ppermute | solution.py:20
  503.1 16.6 %collective-permute-start = (bf16[312,1536]{1,0:T(8,128)(2,1)S(1)}, bf16[312,1536]{1,0:T(8,128)(2,1)S(1)}, u32[]{:S(2)}, u32[]{:S(2)}) collective-permute-start(bf16[312,1536]{1,0:T(8,128)(2,1)S(1)} %get-tuple-element.350), channel_id=1, source_target_pairs={{1,0},{2,1},{3,2},{4,3},{5,4},{6,5},{7,6},{8,7},{9,8},{10,9},{11,1... | collective-permute-start | bytes 2875400 | tf_op jit(solution)/shard_map/while/body/eval_jaxpr/ppermute | solution.py:20
  521.3 16.5 %collective-permute-start = (bf16[312,1536]{1,0:T(8,128)(2,1)S(1)}, bf16[312,1536]{1,0:T(8,128)(2,1)S(1)}, u32[]{:S(2)}, u32[]{:S(2)}) collective-permute-start(bf16[312,1536]{1,0:T(8,128)(2,1)S(1)} %get-tuple-element.350), channel_id=1, source_target_pairs={{1,0},{2,1},{3,2},{4,3},{5,4},{6,5},{7,6},{8,7},{9,8},{10,9},{11,1... | collective-permute-start | bytes 2875400 | tf_op jit(solution)/shard_map/while/body/eval_jaxpr/ppermute | solution.py:20
  539.4 16.6 %collective-permute-start = (bf16[312,1536]{1,0:T(8,128)(2,1)S(1)}, bf16[312,1536]{1,0:T(8,128)(2,1)S(1)}, u32[]{:S(2)}, u32[]{:S(2)}) collective-permute-start(bf16[312,1536]{1,0:T(8,128)(2,1)S(1)} %get-tuple-element.350), channel_id=1, source_target_pairs={{1,0},{2,1},{3,2},{4,3},{5,4},{6,5},{7,6},{8,7},{9,8},{10,9},{11,1... | collective-permute-start | bytes 2875400 | tf_op jit(solution)/shard_map/while/body/eval_jaxpr/ppermute | solution.py:20
  557.6 16.5 %collective-permute-start = (bf16[312,1536]{1,0:T(8,128)(2,1)S(1)}, bf16[312,1536]{1,0:T(8,128)(2,1)S(1)}, u32[]{:S(2)}, u32[]{:S(2)}) collective-permute-start(bf16[312,1536]{1,0:T(8,128)(2,1)S(1)} %get-tuple-element.350), channel_id=1, source_target_pairs={{1,0},{2,1},{3,2},{4,3},{5,4},{6,5},{7,6},{8,7},{9,8},{10,9},{11,1... | collective-permute-start | bytes 2875400 | tf_op jit(solution)/shard_map/while/body/eval_jaxpr/ppermute | solution.py:20
  575.6 16.7 %collective-permute-start = (bf16[312,1536]{1,0:T(8,128)(2,1)S(1)}, bf16[312,1536]{1,0:T(8,128)(2,1)S(1)}, u32[]{:S(2)}, u32[]{:S(2)}) collective-permute-start(bf16[312,1536]{1,0:T(8,128)(2,1)S(1)} %get-tuple-element.350), channel_id=1, source_target_pairs={{1,0},{2,1},{3,2},{4,3},{5,4},{6,5},{7,6},{8,7},{9,8},{10,9},{11,1... | collective-permute-start | bytes 2875400 | tf_op jit(solution)/shard_map/while/body/eval_jaxpr/ppermute | solution.py:20
  593.8 16.6 %collective-permute-start = (bf16[312,1536]{1,0:T(8,128)(2,1)S(1)}, bf16[312,1536]{1,0:T(8,128)(2,1)S(1)}, u32[]{:S(2)}, u32[]{:S(2)}) collective-permute-start(bf16[312,1536]{1,0:T(8,128)(2,1)S(1)} %get-tuple-element.350), channel_id=1, source_target_pairs={{1,0},{2,1},{3,2},{4,3},{5,4},{6,5},{7,6},{8,7},{9,8},{10,9},{11,1... | collective-permute-start | bytes 2875400 | tf_op jit(solution)/shard_map/while/body/eval_jaxpr/ppermute | solution.py:20
  (2 other events, 18.6 us)
Sparse Core Ops, SparseCore 0:
  629.0 151.6 reduce-scatter.3
